TPU v7x, 32 devices: a whole 2x2x4 slice. The times are simulated.
32 devices in a mesh: seq: 4 (over x, core), dp: 8 (over z, y).
Axes of the slice: x: 2, y: 2, z: 4, core: 2. Of those that a mesh axis runs over, the one named last changes fastest.
Arguments:
- tokens: bfloat16 [8, 2048, 2048], P('dp', 'seq'), may hold values from -6 to 6
- log_decay: float32 [8, 8, 2048], P('dp', None, 'seq'), may hold values from -1 to 0
- w_qkv: bfloat16 [2048, 3072], P('dp'), may hold values from -0.125 to 0.125
- w_gate: bfloat16 [2048, 1024], P('dp'), may hold values from -0.125 to 0.125
- w_out: bfloat16 [1024, 2048], P('dp'), may hold values from -0.1875 to 0.1875
- norm_gain: float32 [1024], replicated, may hold values from 0.1 to 1.9
Outputs:
- mixed_rows: bfloat16 [8, 2048, 2048], P('dp', 'seq')
All inputs are finite; a program needn't handle non-finite values.
Results may differ from a plain program's by a relative error of at most 0.0065.
Values may be sent and summed in bfloat16 or wider, within the bound.
A program may use at most 64 MiB of HBM per device.

v0:
```python
import jax
import jax.numpy as jnp
from jax import lax
from jax.sharding import PartitionSpec as P


def fold_states(carried, piece, before, block_totals, my_index):
    span = piece.shape[0]
    mine = lax.dynamic_index_in_dim(before, my_index, 0, keepdims=False)
    order = jnp.arange(span, dtype=jnp.int32)
    earlier = (order < my_index)[:, None]
    decay_gap = mine[None, :] - before - block_totals
    factor = jnp.where(earlier, jnp.exp(jnp.where(earlier, decay_gap, 0.0)), 0.0)
    return carried + jnp.einsum("jh,jhde->hde", factor, piece, precision=lax.Precision.HIGHEST)


def body(tokens, log_decay, w_qkv, w_gate, w_out, norm_gain):
    tok_rows = tokens[0]
    tok_count = tok_rows.shape[0]
    head_count = log_decay.shape[1]
    feat_count = norm_gain.shape[0]
    head_dim = feat_count // head_count
    seq_count = lax.axis_size("seq")
    seq_index = lax.axis_index("seq")
    qkv_width = w_qkv.shape[1] // seq_count
    gate_width = w_gate.shape[1] // seq_count
    slab_width = qkv_width + gate_width
    qkv_slab = lax.dynamic_slice_in_dim(w_qkv, seq_index * qkv_width, qkv_width, 1)
    gate_slab = lax.dynamic_slice_in_dim(w_gate, seq_index * gate_width, gate_width, 1)
    column_slab = jnp.concatenate([qkv_slab, gate_slab], axis=1)
    full_rows = lax.all_gather(column_slab, "dp", axis=0, tiled=True)
    piece = lax.all_gather(full_rows, "seq", axis=1, tiled=True)
    slab_count = piece.shape[1] // slab_width
    product = jnp.dot(tok_rows, piece, preferred_element_type=jnp.float32).reshape(
        tok_count, slab_count, slab_width
    )
    qkv_total = product[:, :, :qkv_width]
    gate_total = product[:, :, qkv_width:]
    projected = qkv_total.reshape(tok_count, seq_count * qkv_width)
    gate_pre = gate_total.reshape(tok_count, seq_count * gate_width)
    activated = (
        jax.nn.silu(projected).astype(jnp.bfloat16).reshape(tok_count, 3, head_count, head_dim)
    )
    query_rows = activated[:, 0]
    key_rows = activated[:, 1]
    value_rows = activated[:, 2]
    cum_decay = jnp.cumsum(log_decay[0], axis=1)
    block_decay = cum_decay[:, -1]
    key_factor = jnp.exp(block_decay[:, None] - cum_decay).T
    scaled_key = (key_rows.astype(jnp.float32) * key_factor[:, :, None]).astype(jnp.bfloat16)
    local_state = jnp.einsum(
        "thd,the->hde", scaled_key, value_rows, preferred_element_type=jnp.float32
    )
    my_index = lax.axis_index("seq")
    empty_state = jnp.zeros((head_count, head_dim, head_dim), jnp.float32)
    all_states, all_decays = (
        lax.all_gather(local_state[None].astype(jnp.bfloat16), "seq", axis=0, tiled=True).astype(
            jnp.float32
        ),
        lax.all_gather(block_decay[None].astype(jnp.bfloat16), "seq", axis=0, tiled=True).astype(
            jnp.float32
        ),
    )
    before = jnp.cumsum(all_decays, axis=0) - all_decays
    carried = fold_states(empty_state, all_states, before, all_decays, my_index)
    scores = jnp.einsum("thd,shd->hts", query_rows, key_rows, preferred_element_type=jnp.float32)
    positions = jnp.arange(tok_count, dtype=jnp.int32)
    causal_mask = (positions[None, :] <= positions[:, None])[None, :, :]
    decay_gap = cum_decay[:, :, None] - cum_decay[:, None, :]
    decay_mat = jnp.where(causal_mask, jnp.exp(jnp.where(causal_mask, decay_gap, 0.0)), 0.0)
    weighted = (scores * decay_mat).astype(jnp.bfloat16)
    intra_part = jnp.einsum(
        "hts,shd->thd", weighted, value_rows, preferred_element_type=jnp.float32
    )
    query_scaled = query_rows.astype(jnp.float32) * jnp.exp(cum_decay).T[:, :, None]
    inter_part = jnp.einsum("thd,hde->the", query_scaled, carried, precision=lax.Precision.HIGHEST)
    attended = (intra_part + inter_part).reshape(tok_count, feat_count)
    mean_square = jnp.mean(attended * attended, axis=1, keepdims=True)
    normed = attended * lax.rsqrt(mean_square + 1e-06) * norm_gain
    gated = (normed * jax.nn.sigmoid(gate_pre)).astype(jnp.bfloat16)
    out_sum = jnp.dot(
        gated, lax.all_gather(w_out, "dp", axis=0, tiled=True), preferred_element_type=jnp.float32
    )
    return out_sum.astype(jnp.bfloat16)[None]


def solution(mesh):
    placed = (
        P("dp", "seq", None),
        P("dp", None, "seq"),
        P("dp", None),
        P("dp", None),
        P("dp", None),
        P(),
    )
    return jax.shard_map(
        body, mesh=mesh, in_specs=placed, out_specs=P("dp", "seq", None), check_vma=False
    )
```

profile of v0, /device:TPU:0, one launch (start us, length us, event | category | flops | bytes accessed | tf_op | source)
XLA Modules:
  0.0 327.2 jit_solution(16576440834460175521)
XLA Ops:
  6.5 1.2 constant_dynamic-slice_fusion.2
  7.7 0.9 constant_dynamic-slice_fusion.1
  8.7 0.9 pad_maximum_fusion
  9.6 75.6 %all-gather.7.cloned.1.call-done = bf16[2048,1024]{1,0:T(8,128)(2,1)} async-done(((bf16[256,1024]{1,0:T(8,128)(2,1)}), bf16[2048,1024]{1,0:T(8,128)(2,1)}) %all-gather.7.cloned.1.call-update) | async-done | bytes 4194320 | tf_op jit(solution)/shard_map/all_gather | solution.py:31
  85.3 1.1 reduce-window.6
  87.0 104.2 %all-gather.9.cloned.1.call-done = bf16[2048,4096]{1,0:T(8,128)(2,1)} async-done(((bf16[2048,1024]{1,0:T(8,128)(2,1)}), bf16[2048,4096]{1,0:T(8,128)(2,1)}) %all-gather.9.cloned.1.call-update) | async-done | bytes 16777232 | tf_op jit(solution)/shard_map/all_gather | solution.py:32
  191.2 11.7 %fusion.12 = f32[4096,512]{1,0:T(8,128)S(1)} fusion(bf16[2048,4096]{1,0:T(8,128)(2,1)} %all-gather.9.cloned.1.call-done, bf16[1,512,2048]{2,1,0:T(8,128)(2,1)S(1)} %copy-done), kind=kOutput, calls=%fused_computation.17 | convolution fusion | flops 8589934592 | bytes 27262976 | tf_op jit(solution)/shard_map/dot_general | solution.py:34
  203.0 3.8 %slice.32 = f32[512,4,768]{0,2,1:T(8,128)} slice(f32[512,4,1024]{0,2,1:T(8,128)S(1)} %bitcast.65), slice={[0:512], [0:4], [0:768]} | slice | bytes 12582912 | tf_op jit(solution)/shard_map/slice | solution.py:37
  206.8 1.3 copy-done.1
  208.1 6.6 %copy.22 = f32[512,3,8,128]{3,0,2,1:T(8,128)} copy(f32[512,3,8,128]{0,3,2,1:T(8,128)} %bitcast.64) | data formatting | bytes 12582912 | tf_op jit(solution)/shard_map/reshape | solution.py:39
  214.7 4.4 %multiply_convert_fusion.1 = bf16[512,3,8,128]{3,0,2,1:T(8,128)(2,1)S(1)} fusion(f32[512,3,8,128]{3,0,2,1:T(8,128)} %copy.22), kind=kLoop, calls=%fused_computation.1 | loop fusion | flops 7864320 | bytes 9437184 | tf_op jit(solution)/shard_map/convert_element_type | solution.py:42
  219.1 1.7 copy-done.3
  220.8 2.3 convolution_convert_fusion.1
  223.2 0.5 all-gather.11.cloned.1.call-update
  223.7 0.6 dynamic-slice
  225.1 0.2 dynamic-update-slice
  225.4 6.1 %all-reduce = bf16[32]{0:T(256)(128)(2,1)S(1)} all-reduce(bf16[32]{0:T(256)(128)(2,1)S(1)} %dynamic-update-slice), channel_id=2, replica_groups=mesh['seq'=4,'dp'=8] {'seq'}, use_global_device_ids=true, to_apply=%add | all-reduce | flops 32 | bytes 128
  231.8 3.5 %fusion.7 = f32[512,4,256]{0,2,1:T(8,128)} fusion(f32[512,4,1024]{0,2,1:T(8,128)} %bitcast.66), kind=kLoop, calls=%fused_computation.10 | loop fusion | flops 1572864 | bytes 4194304 | tf_op jit(solution)/shard_map/div | solution.py:80
  235.2 6.7 %fusion = f32[8,128,512]{2,1,0:T(8,128)} fusion(f32[8,512]{1,0:T(8,128)S(1)} %get-tuple-element.6, pred[512,512]{1,0:T(8,128)(4,1)S(1)} %iota_compare_fusion, bf16[512,3,8,128]{3,0,2,1:T(8,128)(2,1)} %copy-done.3), kind=kOutput, calls=%fused_computation.2 | convolution fusion | flops 1084227584 | bytes 5537792 | tf_op jit(solution)/shard_map/hts,shd->thd/dot_general | solution.py:72
  242.0 1.6 multiply_reduce_fusion
  243.6 4.8 %fusion.11 = (f32[512]{0:T(512)S(1)}, f32[8,128,512]{2,1,0:T(8,128)S(1)}) fusion(f32[8,128,512]{2,1,0:T(8,128)} %fusion, f32[8,128,128]{2,1,0:T(8,128)S(1)} %multiply_reduce_fusion, f32[512,8]{0,1:T(8,128)S(1)} %get-tuple-element.5, bf16[512,3,8,128]{3,0,2,1:T(8,128)(2,1)} %copy-done.3), kind=kOutput, calls=%fused_computation.16 | convolution fusion | flops 807927296 | bytes 5785600 | tf_op jit(solution)/shard_map/thd,hde->the/dot_general | solution.py:76
  248.4 0.3 fusion.10
  248.7 66.0 %all-gather.11.cloned.1.call-done = bf16[1024,2048]{1,0:T(8,128)(2,1)} async-done(((bf16[128,2048]{1,0:T(8,128)(2,1)}), bf16[1024,2048]{1,0:T(8,128)(2,1)}) %all-gather.11.cloned.1.call-update) | async-done | bytes 4194320 | tf_op jit(solution)/shard_map/all_gather | solution.py:82
  314.8 5.9 %fusion.4 = bf16[1,512,2048]{2,1,0:T(8,128)(2,1)} fusion(bf16[512,1024]{0,1:T(8,128)(2,1)S(1)} %fusion.10, bf16[1024,2048]{1,0:T(8,128)(2,1)} %all-gather.11.cloned.1.call-done), kind=kOutput, calls=%fused_computation.6 | convolution fusion | flops 2148532224 | bytes 7340032 | tf_op jit(solution)/shard_map/dot_general | solution.py:81
  (36 shorter events, 1.2 us)
Async XLA Ops:
  6.5 184.7 %copy-start = (bf16[1,512,2048]{2,1,0:T(8,128)(2,1)S(1)}, bf16[1,512,2048]{2,1,0:T(8,128)(2,1)}, u32[]{:S(2)}) copy-start(bf16[1,512,2048]{2,1,0:T(8,128)(2,1)} %param.6) | copy-start | bytes 6291460
  6.5 78.7 %all-gather.7.cloned.1.call-start = ((), (), s32[]{:S(2)}) async-start(), calls=%async_computation | async-start | bytes 4718592 | tf_op jit(solution)/shard_map/all_gather | solution.py:31
  7.7 77.6 %copy-start.4 = (f32[1,8,512]{2,1,0:T(8,128)S(1)}, f32[1,8,512]{2,1,0:T(8,128)}, u32[]{:S(2)}) copy-start(f32[1,8,512]{2,1,0:T(8,128)} %param.7) | copy-start | bytes 49156
  9.5 181.7 %all-gather.9.cloned.1.call-start = ((), (), s32[]{:S(2)}) async-start(), calls=%async_computation.1 | async-start | bytes 20971520 | tf_op jit(solution)/shard_map/all_gather | solution.py:32
  85.2 156.7 %all-gather.13.cloned.1.call-start = ((), (), s32[]{:S(2)}) async-start(), calls=%async_computation.3 | async-start | bytes 1310720 | tf_op jit(solution)/shard_map/all_gather | solution.py:57
  203.0 5.1 %copy-start.1 = (f32[4096,512]{1,0:T(8,128)}, f32[4096,512]{1,0:T(8,128)S(1)}, u32[]{:S(2)}) copy-start(f32[4096,512]{1,0:T(8,128)S(1)} %fusion.12) | copy-start | bytes 25165828
  219.1 1.7 copy-start.3
  220.8 2.9 copy-start.6
  223.1 91.7 %all-gather.11.cloned.1.call-start = ((), (), s32[]{:S(2)}) async-start(), calls=%async_computation.2 | async-start | bytes 4718592 | tf_op jit(solution)/shard_map/all_gather | solution.py:82
  243.5 4.9 %copy-start.2 = (f32[512,4,256]{0,2,1:T(8,128)S(1)}, f32[512,4,256]{0,2,1:T(8,128)}, u32[]{:S(2)}) copy-start(f32[512,4,256]{0,2,1:T(8,128)} %fusion.7) | copy-start | bytes 6291460
  243.5 4.9 %copy-start.5 = (f32[1024]{0:T(1024)S(1)}, f32[1024]{0:T(1024)}, u32[]{:S(2)}) copy-start(f32[1024]{0:T(1024)} %param.11) | copy-start | bytes 12292
Sparse Core Ops, SparseCore 0:
  9.7 75.5 all-gather.6
  86.8 104.4 all-gather.8
  223.2 16.6 all-gather.12
  241.9 72.7 all-gather.10
where the time goes:
time: 328 us; the launch traced here: 327 us
  waiting for transfers between devices  246 us (75%)
  matrix products  31.5 us (10%)
  local copies, waits for them, and re-layouts  16.9 us (5%)
  between operations  13.9 us (4%)
  other arithmetic  12.2 us (4%)
  blocking collectives  6.06 us (2%)
    all_gather x1, waiting for transfers between devices, body(): piece = lax.all_gather(full_rows, 'seq', axis=1, tiled=True)  104 us
    all_gather x1, waiting for transfers between devices, body(): full_rows = lax.all_gather(column_slab, 'dp', axis=0, tiled=True)  75.6 us
    all_gather x1, waiting for transfers between devices, body(): lax.all_gather(w_out, 'dp', axis=0, tiled=True)  66 us
    dot_general x1, matrix products, body(): jnp.dot(tok_rows, piece, preferred_element_type=jnp.float32)  11.7 us
    dot_general x1, matrix products, body(): jnp.einsum('hts,shd->thd', weighted, value_rows, preferred_element_type=j...  6.75 us
    reshape x1, local copies, waits for them, and re-layouts, body(): projected = qkv_total.reshape(tok_count, seq_count * qkv_width)  6.59 us
  transfers between devices with their start and end apart: 4, of which 3 were waited for; matrix products, arithmetic and copies ran while one was open for 6% of the time, Pallas kernels for 0%

commit v1 on v0

--- a/solution.py
+++ b/solution.py
@@ -2,6 +2,13 @@
 import jax.numpy as jnp
 from jax import lax
 from jax.sharding import PartitionSpec as P
+
+match_the_files = lambda row_data, chip_axis: jnp.concatenate(
+    lax.all_to_all(
+        jnp.stack([row_data for _ in range(lax.axis_size(chip_axis))], 0), chip_axis, 0, 0
+    ),
+    0,
+)
 
 
 def fold_states(carried, piece, before, block_totals, my_index):
@@ -78,9 +85,7 @@
     mean_square = jnp.mean(attended * attended, axis=1, keepdims=True)
     normed = attended * lax.rsqrt(mean_square + 1e-06) * norm_gain
     gated = (normed * jax.nn.sigmoid(gate_pre)).astype(jnp.bfloat16)
-    out_sum = jnp.dot(
-        gated, lax.all_gather(w_out, "dp", axis=0, tiled=True), preferred_element_type=jnp.float32
-    )
+    out_sum = jnp.dot(gated, match_the_files(w_out, "dp"), preferred_element_type=jnp.float32)
     return out_sum.astype(jnp.bfloat16)[None]
 
 

time: 328 us -> 262 us (0.80)
  waiting for transfers between devices: 246 us -> 173 us
  starting transfers between devices: 0.12 us -> 4.77 us
    all_gather x1 -> x0, waiting for transfers between devices: 66 us -> none  [body(): lax.all_gather(w_out, 'dp', axis=0, tiled=True)]
    all_gather x1, waiting for transfers between devices: 104 us -> 96.8 us  [body(): piece = lax.all_gather(full_rows, 'seq', axis=1, tiled=True)]
    all_to_all x0 -> x1, starting transfers between devices: none -> 4.68 us  [lax.all_to_all(jnp.stack([row_data for _ in range(lax.axis_size(chip_axis...]
  transfers between devices with their start and end apart: 4 -> 4, of which waited for: 3 -> 2; matrix products, arithmetic and copies ran while one was open for 6% -> 19% of each run, Pallas kernels for 0% -> 0%
where the time goes in v1:
time: 262 us; the launch traced here: 261 us
  waiting for transfers between devices  173 us (66%)
  matrix products  32.3 us (12%)
  local copies, waits for them, and re-layouts  19.7 us (8%)
  between operations  13.9 us (5%)
  other arithmetic  12 us (5%)
  blocking collectives  6.06 us (2%)
  starting transfers between devices  4.77 us (2%)
    all_gather x1, waiting for transfers between devices, body(): piece = lax.all_gather(full_rows, 'seq', axis=1, tiled=True)  96.8 us
    all_gather x1, waiting for transfers between devices, body(): full_rows = lax.all_gather(column_slab, 'dp', axis=0, tiled=True)  75.6 us
    dot_general x1, matrix products, body(): jnp.dot(tok_rows, piece, preferred_element_type=jnp.float32)  11.7 us
    dot_general x1, matrix products, body(): jnp.dot(gated, match_the_files(w_out, 'dp'), preferred_element_type=jnp.f...  7.55 us
    reshape x1, local copies, waits for them, and re-layouts, body(): projected = qkv_total.reshape(tok_count, seq_count * qkv_width)  6.59 us
    unnamed x1, blocking collectives  6.06 us
    dot_general x1, matrix products, body(): jnp.einsum('hts,shd->thd', weighted, value_rows, preferred_element_type=j...  5.44 us
  transfers between devices with their start and end apart: 4, of which 2 were waited for; matrix products, arithmetic and copies ran while one was open for 19% of the time, Pallas kernels for 0%

profile of v1, /device:TPU:0, one launch (start us, length us, event | category | flops | bytes accessed | tf_op | source)
XLA Modules:
  0.0 261.1 jit_solution(3857105149696081816)
XLA Ops:
  6.5 1.2 constant_dynamic-slice_fusion.2
  7.7 1.0 constant_dynamic-slice_fusion.1
  8.7 0.9 pad_maximum_fusion
  9.6 75.6 %all-gather.6.cloned.1.call-done = bf16[2048,1024]{1,0:T(8,128)(2,1)} async-done(((bf16[256,1024]{1,0:T(8,128)(2,1)}), bf16[2048,1024]{1,0:T(8,128)(2,1)}) %all-gather.6.cloned.1.call-update) | async-done | bytes 4194320 | tf_op jit(solution)/shard_map/all_gather | solution.py:38
  85.3 2.5 stack.2
  87.8 4.7 %all-to-all-start = ((bf16[8,128,2048]{2,1,0:T(8,128)(2,1)}), bf16[8,128,2048]{2,1,0:T(8,128)(2,1)}, u32[]{:S(2)}, u32[]{:S(2)}) async-start(bf16[8,128,2048]{2,1,0:T(8,128)(2,1)} %stack.2), calls=%async_computation | async-start | bytes 8388608 | tf_op jit(solution)/shard_map/all_to_all | solution.py:7
  92.6 1.1 reduce-window.6
  94.0 0.2 fusion.22
  94.5 96.8 %all-gather.8.cloned.1.call-done = bf16[2048,4096]{1,0:T(8,128)(2,1)} async-done(((bf16[2048,1024]{1,0:T(8,128)(2,1)}), bf16[2048,4096]{1,0:T(8,128)(2,1)}) %all-gather.8.cloned.1.call-update) | async-done | bytes 16777232 | tf_op jit(solution)/shard_map/all_gather | solution.py:39
  191.3 11.7 %fusion.9 = f32[4096,512]{1,0:T(8,128)S(1)} fusion(bf16[2048,4096]{1,0:T(8,128)(2,1)} %all-gather.8.cloned.1.call-done, bf16[1,512,2048]{2,1,0:T(8,128)(2,1)S(1)} %copy-done), kind=kOutput, calls=%fused_computation.13 | convolution fusion | flops 8589934592 | bytes 27262976 | tf_op jit(solution)/shard_map/dot_general | solution.py:41
  203.0 3.8 %slice.32 = f32[512,4,768]{0,2,1:T(8,128)} slice(f32[512,4,1024]{0,2,1:T(8,128)S(1)} %bitcast.61), slice={[0:512], [0:4], [0:768]} | slice | bytes 12582912 | tf_op jit(solution)/shard_map/slice | solution.py:44
  206.9 1.3 copy-done.2
  208.2 6.6 %copy.26 = f32[512,3,8,128]{3,0,2,1:T(8,128)} copy(f32[512,3,8,128]{0,3,2,1:T(8,128)} %bitcast.59) | data formatting | bytes 12582912 | tf_op jit(solution)/shard_map/reshape | solution.py:46
  214.7 4.4 %multiply_convert_fusion.1 = bf16[512,3,8,128]{3,0,2,1:T(8,128)(2,1)S(1)} fusion(f32[512,3,8,128]{3,0,2,1:T(8,128)} %copy.26), kind=kLoop, calls=%fused_computation.1 | loop fusion | flops 7864320 | bytes 9437184 | tf_op jit(solution)/shard_map/convert_element_type | solution.py:49
  219.2 1.7 copy-done.3
  220.9 2.3 convolution_convert_fusion
  223.3 0.6 dynamic-slice
  224.5 0.2 dynamic-update-slice
  224.8 6.1 %all-reduce = bf16[32]{0:T(256)(128)(2,1)S(1)} all-reduce(bf16[32]{0:T(256)(128)(2,1)S(1)} %dynamic-update-slice), channel_id=2, replica_groups=mesh['seq'=4,'dp'=8] {'seq'}, use_global_device_ids=true, to_apply=%add | all-reduce | flops 32 | bytes 128
  231.1 3.6 %fusion.7 = f32[512,4,256]{0,2,1:T(8,128)} fusion(f32[512,4,1024]{0,2,1:T(8,128)} %bitcast.62), kind=kLoop, calls=%fused_computation.10 | loop fusion | flops 1572864 | bytes 4194304 | tf_op jit(solution)/shard_map/div | solution.py:87
  234.7 5.4 %fusion = f32[8,128,512]{2,1,0:T(8,128)S(1)} fusion(f32[8,512]{1,0:T(8,128)S(1)} %get-tuple-element.6, pred[512,512]{1,0:T(8,128)(4,1)S(1)} %iota_compare_fusion, bf16[512,3,8,128]{3,0,2,1:T(8,128)(2,1)} %copy-done.3), kind=kOutput, calls=%fused_computation.3 | convolution fusion | flops 1084227584 | bytes 5537792 | tf_op jit(solution)/shard_map/hts,shd->thd/dot_general | solution.py:79
  240.2 1.6 multiply_reduce_fusion
  241.8 5.2 %multiply_reduce_fusion.1 = (f32[512]{0:T(512)S(1)}, f32[8,128,512]{2,1,0:T(8,128)}) fusion(f32[8,128,512]{2,1,0:T(8,128)S(1)} %fusion, f32[8,128,128]{2,1,0:T(8,128)S(1)} %multiply_reduce_fusion, f32[512,8]{0,1:T(8,128)S(1)} %get-tuple-element.5, bf16[512,3,8,128]{3,0,2,1:T(8,128)(2,1)} %copy-done.3), kind=kOutput, calls=%fused_computation.16 | convolution fusion | flops 807927296 | bytes 5785600 | tf_op jit(solution)/shard_map/thd,hde->the/dot_general | solution.py:83
  247.0 7.6 %fusion.4 = bf16[1,512,2048]{2,1,0:T(8,128)(2,1)} fusion(bf16[8,128,2048]{2,1,0:T(8,128)(2,1)} %all-to-all-done, f32[512,8,128]{0,2,1:T(8,128)} %bitcast.60, f32[8,128,512]{2,1,0:T(8,128)} %get-tuple-element.8, f32[8,128]{1,0:T(8,128)S(1)} %bitcast.64, f32[512]{0:T(512)S(1)} %add_rsqrt_fusion), kind=kOutput, calls=%fused_computation.6 | convolution fusion | flops 2150629376 | bytes 10491904 | tf_op jit(solution)/shard_map/dot_general | solution.py:88
  (37 shorter events, 1.0 us)
Async XLA Ops:
  6.5 184.7 %copy-start = (bf16[1,512,2048]{2,1,0:T(8,128)(2,1)S(1)}, bf16[1,512,2048]{2,1,0:T(8,128)(2,1)}, u32[]{:S(2)}) copy-start(bf16[1,512,2048]{2,1,0:T(8,128)(2,1)} %param.6) | copy-start | bytes 6291460
  6.5 78.7 %all-gather.6.cloned.1.call-start = ((), (), s32[]{:S(2)}) async-start(), calls=%async_computation.1 | async-start | bytes 4718592 | tf_op jit(solution)/shard_map/all_gather | solution.py:38
  7.7 77.6 %copy-start.4 = (bf16[128,2048]{1,0:T(8,128)(2,1)S(1)}, bf16[128,2048]{1,0:T(8,128)(2,1)}, u32[]{:S(2)}) copy-start(bf16[128,2048]{1,0:T(8,128)(2,1)} %param.10) | copy-start | bytes 1572868
  9.6 181.7 %all-gather.8.cloned.1.call-start = ((), (), s32[]{:S(2)}) async-start(), calls=%async_computation.2 | async-start | bytes 20971520 | tf_op jit(solution)/shard_map/all_gather | solution.py:39
  87.8 4.7 %copy-start.6 = (f32[1,8,512]{2,1,0:T(8,128)S(1)}, f32[1,8,512]{2,1,0:T(8,128)}, u32[]{:S(2)}) copy-start(f32[1,8,512]{2,1,0:T(8,128)} %param.7) | copy-start | bytes 49156
  87.8 159.2 %all-to-all-start = ((bf16[8,128,2048]{2,1,0:T(8,128)(2,1)}), bf16[8,128,2048]{2,1,0:T(8,128)(2,1)}, u32[]{:S(2)}, u32[]{:S(2)}) async-start(bf16[8,128,2048]{2,1,0:T(8,128)(2,1)} %stack.2), calls=%async_computation | async-start | bytes 8388608 | tf_op jit(solution)/shard_map/all_to_all | solution.py:7
  92.5 147.7 %all-gather.10.cloned.1.call-start = ((), (), s32[]{:S(2)}) async-start(), calls=%async_computation.3 | async-start | bytes 1310720 | tf_op jit(solution)/shard_map/all_gather | solution.py:64
  203.0 5.1 %copy-start.2 = (f32[4096,512]{1,0:T(8,128)}, f32[4096,512]{1,0:T(8,128)S(1)}, u32[]{:S(2)}) copy-start(f32[4096,512]{1,0:T(8,128)S(1)} %fusion.9) | copy-start | bytes 25165828
  219.2 1.8 copy-start.3
  220.9 2.3 copy-start.7
  241.8 5.3 %copy-start.5 = (f32[1024]{0:T(1024)S(1)}, f32[1024]{0:T(1024)}, u32[]{:S(2)}) copy-start(f32[1024]{0:T(1024)} %param.11) | copy-start | bytes 12292
  247.0 7.6 %copy-start.1 = (bf16[1,512,2048]{2,1,0:T(8,128)(2,1)S(1)}, bf16[1,512,2048]{2,1,0:T(8,128)(2,1)}, u32[]{:S(2)}) copy-start(bf16[1,512,2048]{2,1,0:T(8,128)(2,1)} %param.6) | copy-start | bytes 6291460
Sparse Core Ops, SparseCore 0:
  9.7 75.5 all-gather.5
  86.8 104.4 all-gather.7
  223.4 16.6 all-gather.9
